TPU v7x, 128 devices: a whole 4x4x4 slice. The times are simulated.
128 devices in a mesh: dp: 8 (over y, core), adapter: 16 (over x, z).
Axes of the slice: x: 4, y: 4, z: 4, core: 2. Of those that a mesh axis runs over, the one named last changes fastest.
Arguments:
- activations: bfloat16 [8192, 28672], P('adapter', 'dp'), may hold values from -6 to 6
- cotangent: bfloat16 [8192, 8192], P('adapter', 'dp'), may hold values from -6 to 6
- factor_in: bfloat16 [512, 16, 28672], P('adapter', None, 'dp'), may hold values from -0.03125 to 0.03125
- factor_out: bfloat16 [512, 16, 8192], P('adapter', None, 'dp'), may hold values from -0.0625 to 0.0625
- adapter_ids: int32 [32, 8], P('adapter'), may hold values from 0 to 511, as said below
- router_weights: float32 [32, 8], P('adapter'), may hold values from 0.25 to 1
Outputs:
- input_grad: float32 [8192, 28672], P('adapter', 'dp')
- grad_factor_in: bfloat16 [512, 16, 28672], P('adapter', None, 'dp')
- grad_factor_out: bfloat16 [512, 16, 8192], P('adapter', None, 'dp')
- router_grad: float32 [32, 8], P('adapter')
Inputs may be any that keep to these rules, and one draw needn't show every extreme that they name: `adapter_ids`: the 8 adapters of a request are different. The owner of adapter e is e // 32. Requests are taken in aligned groups of 2 (those of one index of adapter); among the 16 adapters named by one group no owner holds more than 2, and in every group some owner holds exactly 2.
All inputs are finite; a program needn't handle non-finite values.
Results may differ from a plain program's by a relative error of at most 0.012.
Values may be sent and summed in bfloat16 or wider, within the bound.
A program may use at most 128 MiB of HBM per device.

v0:
```python
import jax
import jax.numpy as jnp
from jax import lax
from jax.sharding import PartitionSpec as P

CAP = 2


def body(activations, cotangent, factor_in, factor_out, adapter_ids, router_weights):
    owner_count = lax.axis_size("adapter")
    my_index = lax.axis_index("adapter")
    exp_count = factor_in.shape[0]
    rank_width = factor_in.shape[1]
    req_count = adapter_ids.shape[0]
    top_count = adapter_ids.shape[1]
    pair_count = req_count * top_count
    length = activations.shape[0] // req_count
    slot_count = owner_count * CAP
    my_pairs = adapter_ids.reshape(pair_count)
    my_owner = my_pairs // exp_count
    before = jnp.arange(pair_count)[:, None] > jnp.arange(pair_count)[None, :]
    my_slot = jnp.sum((my_owner[:, None] == my_owner[None, :]) & before, axis=1)
    target = my_owner * CAP + my_slot
    picker = target[:, None] == jnp.arange(slot_count)[None, :]
    all_ids = lax.all_gather(adapter_ids, "adapter", axis=0, tiled=True).reshape(
        owner_count, pair_count
    )
    all_owner = all_ids // exp_count
    all_slot = jnp.sum(
        (all_owner[:, :, None] == all_owner[:, None, :]) & before[None, :, :], axis=2
    )
    is_mine = all_owner == my_index
    local_idx = all_ids - my_index * exp_count
    matches = (
        is_mine[:, :, None, None]
        & (all_slot[:, :, None, None] == jnp.arange(CAP)[None, None, :, None])
        & (local_idx[:, :, None, None] == jnp.arange(exp_count)[None, None, None, :])
    )
    selector = jnp.any(matches, axis=1)
    selector = selector.astype(jnp.bfloat16)
    send_in = jnp.einsum(
        "jce,erf->jcrf", selector, factor_in, preferred_element_type=jnp.float32
    ).astype(jnp.bfloat16)
    send_out = jnp.einsum(
        "jce,erd->jcrd", selector, factor_out, preferred_element_type=jnp.float32
    ).astype(jnp.bfloat16)
    rows_in = activations.reshape(req_count, length, -1)
    rows_out = cotangent.reshape(req_count, length, -1)
    picker_bf = picker.astype(jnp.bfloat16)
    got_in, got_out = (
        lax.all_to_all(send_in, "adapter", split_axis=0, concat_axis=0, tiled=True),
        lax.all_to_all(send_out, "adapter", split_axis=0, concat_axis=0, tiled=True),
    )
    got_in = got_in.reshape(slot_count, rank_width, -1)
    got_out = got_out.reshape(slot_count, rank_width, -1)
    pair_in = jnp.einsum(
        "qs,srf->qrf", picker_bf, got_in, preferred_element_type=jnp.float32
    ).astype(jnp.bfloat16)
    pair_out = jnp.einsum(
        "qs,srd->qrd", picker_bf, got_out, preferred_element_type=jnp.float32
    ).astype(jnp.bfloat16)
    pair_in = pair_in.reshape(req_count, top_count * rank_width, -1)
    pair_out = pair_out.reshape(req_count, top_count * rank_width, -1)
    part_proj = jnp.einsum("blf,bjf->blj", rows_in, pair_in, preferred_element_type=jnp.float32)
    part_pull = jnp.einsum("bld,bjd->blj", rows_out, pair_out, preferred_element_type=jnp.float32)
    projected, pulled = lax.psum((part_proj, part_pull), "dp")
    router_grad = jnp.sum(
        (projected * pulled).reshape(req_count, length, top_count, rank_width), axis=(1, 3)
    )
    row_scale = jnp.repeat(router_weights, rank_width, axis=1)
    pulled_weighted = (pulled * row_scale[:, None, :]).astype(jnp.bfloat16)
    projected_weighted = (projected * row_scale[:, None, :]).astype(jnp.bfloat16)
    input_grad = jnp.einsum(
        "blj,bjf->blf", pulled_weighted, pair_in, preferred_element_type=jnp.float32
    ).reshape(req_count * length, -1)
    term_in = jnp.einsum(
        "blj,blf->bjf", pulled_weighted, rows_in, preferred_element_type=jnp.float32
    ).astype(jnp.bfloat16)
    term_out = jnp.einsum(
        "blj,bld->bjd", projected_weighted, rows_out, preferred_element_type=jnp.float32
    ).astype(jnp.bfloat16)
    back_in = jnp.einsum(
        "qs,qrf->srf",
        picker_bf,
        term_in.reshape(pair_count, rank_width, -1),
        preferred_element_type=jnp.float32,
    ).astype(jnp.bfloat16)
    back_out = jnp.einsum(
        "qs,qrd->srd",
        picker_bf,
        term_out.reshape(pair_count, rank_width, -1),
        preferred_element_type=jnp.float32,
    ).astype(jnp.bfloat16)
    back_in = back_in.reshape(owner_count, CAP, rank_width, -1)
    back_out = back_out.reshape(owner_count, CAP, rank_width, -1)
    ret_in, ret_out = (
        lax.all_to_all(back_in, "adapter", split_axis=0, concat_axis=0, tiled=True),
        lax.all_to_all(back_out, "adapter", split_axis=0, concat_axis=0, tiled=True),
    )
    grad_factor_in = jnp.einsum(
        "jce,jcrf->erf", selector, ret_in, preferred_element_type=jnp.float32
    ).astype(jnp.bfloat16)
    grad_factor_out = jnp.einsum(
        "jce,jcrd->erd", selector, ret_out, preferred_element_type=jnp.float32
    ).astype(jnp.bfloat16)
    return (input_grad, grad_factor_in, grad_factor_out, router_grad)


def solution(mesh):
    return jax.shard_map(
        body,
        mesh=mesh,
        in_specs=(
            P("adapter", "dp"),
            P("adapter", "dp"),
            P("adapter", None, "dp"),
            P("adapter", None, "dp"),
            P("adapter", None),
            P("adapter", None),
        ),
        out_specs=(
            P("adapter", "dp"),
            P("adapter", None, "dp"),
            P("adapter", None, "dp"),
            P("adapter", None),
        ),
        check_vma=False,
    )
```

profile of v0, /device:TPU:124, one launch (start us, length us, event | category | flops | bytes accessed | tf_op | source)
XLA Modules:
  0.0 286.8 jit_solution(15268726753402709077)
XLA Ops:
  7.2 0.0 copy-start
  7.2 21.6 %all-gather = s32[16,2,8]{2,1,0:T(2,128)S(1)} all-gather(s32[1,2,8]{2,1,0:T(2,128)} %bitcast.82), channel_id=1, replica_groups=mesh['dp'=8,'adapter'=16] {'adapter'}, dimensions={0}, use_global_device_ids=true | all-gather | bytes 1088 | tf_op jit(solution)/shard_map/all_gather | solution.py:25
  28.8 0.1 copy.61
  28.9 0.1 copy.65
  28.9 0.1 copy.62
  29.0 0.1 copy.63
  29.1 0.1 iota_compare_fusion
  29.2 0.4 convert_reduce_fusion
  29.7 0.2 and_reduce_fusion
  29.8 2.7 convolution_convert_fusion.4
  32.5 1.5 copy.68
  34.1 6.9 %all-to-all-start = ((bf16[16,2,16,1024]{3,2,1,0:T(8,128)(2,1)}), bf16[16,2,16,1024]{3,2,1,0:T(8,128)(2,1)S(1)}, u32[]{:S(2)}, u32[]{:S(2)}) async-start(bf16[16,2,16,1024]{3,2,1,0:T(8,128)(2,1)} %copy.68), calls=%async_computation | async-start | bytes 2097152 | tf_op jit(solution)/shard_map/all_to_all | solution.py:52
  41.0 6.9 %convolution_convert_fusion = bf16[16,2,16,3584]{3,0,2,1:T(8,128)(2,1)S(1)} fusion(bf16[32,16,3584]{2,1,0:T(8,128)(2,1)} %param.8, pred[16,2,32,1]{2,1,0,3:T(4,128)(4,1)S(1)} %bitcast.81), kind=kOutput, calls=%fused_computation.1 | convolution fusion | flops 119275520 | bytes 7341056 | tf_op jit(solution)/shard_map/jce,erf->jcrf/dot_general | solution.py:41
  47.9 3.8 %copy.73 = bf16[16,2,16,3584]{3,2,1,0:T(8,128)(2,1)} copy(bf16[16,2,16,3584]{3,0,2,1:T(8,128)(2,1)S(1)} %convolution_convert_fusion) | data formatting | bytes 7340032 | tf_op jit(solution)/shard_map/convert_element_type | solution.py:43
  51.7 7.4 %all-to-all-start.1 = ((bf16[16,2,16,3584]{3,2,1,0:T(8,128)(2,1)}), bf16[16,2,16,3584]{3,2,1,0:T(8,128)(2,1)}, u32[]{:S(2)}, u32[]{:S(2)}) async-start(bf16[16,2,16,3584]{3,2,1,0:T(8,128)(2,1)} %copy.73), calls=%async_computation.1 | async-start | bytes 7340032 | tf_op jit(solution)/shard_map/all_to_all | solution.py:51
  59.1 0.2 all-reduce.3.cloned.1.call-start
  59.3 0.1 reshape.240
  59.4 0.2 convert_reduce_fusion.1
  59.6 1.2 convolution_convert_fusion.7
  60.9 0.3 copy.70
  61.2 1.2 convolution_bitcast_fusion.1
  62.4 39.2 %all-to-all-done.1 = bf16[16,2,16,3584]{3,2,1,0:T(8,128)(2,1)} async-done(((bf16[16,2,16,3584]{3,2,1,0:T(8,128)(2,1)}), bf16[16,2,16,3584]{3,2,1,0:T(8,128)(2,1)}, u32[]{:S(2)}, u32[]{:S(2)}) %all-to-all-start.1) | async-done | bytes 3670048 | tf_op jit(solution)/shard_map/all_to_all | solution.py:51
  101.6 6.2 %convolution_convert_fusion.3 = bf16[16,16,3584]{2,0,1:T(8,128)(2,1)S(1)} fusion(bf16[32,16,3584]{2,1,0:T(8,128)(2,1)} %bitcast.11, s32[16]{0:T(128)S(1)} %multiply_add_fusion), kind=kOutput, calls=%fused_computation.4 | convolution fusion | flops 59638272 | bytes 5505088 | tf_op jit(solution)/shard_map/qs,srf->qrf/dot_general | solution.py:56
  107.8 1.0 copy.75
  108.8 2.0 convolution_bitcast_fusion
  110.8 0.0 all-reduce.3.cloned.1.call-update
  110.9 0.1 broadcast_in_dim.2
  110.9 0.1 mul.31
  111.0 61.1 %all-reduce.3.cloned.1.call-done = (f32[2,256,128]{1,2,0:T(8,128)}, f32[2,256,128]{1,2,0:T(8,128)}) async-done(((f32[2,256,128]{1,2,0:T(8,128)}, f32[2,256,128]{1,2,0:T(8,128)}), (f32[2,256,128]{1,2,0:T(8,128)}, f32[2,256,128]{1,2,0:T(8,128)})) %all-reduce.3.cloned.1.call-update) | async-done | bytes 524304 | tf_op jit(solution)/shard_map/psum | solution.py:66
  172.1 1.3 convolution_convert_fusion.6
  173.5 0.6 convolution_convert_fusion.5
  174.0 1.2 reshape.252
  175.3 3.2 %copy.82 = bf16[16,2,16,1024]{3,1,2,0:T(2,128)(2,1)} copy(bf16[16,2,16,1024]{3,1,0,2:T(2,128)(2,1)} %reshape.252) | data formatting | bytes 2097152 | tf_op jit(solution)/shard_map/reshape | solution.py:95
  178.4 7.1 %all-to-all-start.3 = ((bf16[16,2,16,1024]{3,1,2,0:T(2,128)(2,1)}), bf16[16,2,16,1024]{3,1,2,0:T(2,128)(2,1)S(1)}, u32[]{:S(2)}, u32[]{:S(2)}) async-start(bf16[16,2,16,1024]{3,1,2,0:T(2,128)(2,1)} %copy.82), calls=%async_computation.3 | async-start | bytes 2097152 | tf_op jit(solution)/shard_map/all_to_all | solution.py:98
  185.6 2.7 convolution_convert_fusion.2
  188.3 4.2 %convolution_convert_fusion.1 = bf16[32,16,3584]{2,0,1:T(8,128)(2,1)} fusion(bf16[16,16,3584]{2,1,0:T(8,128)(2,1)S(1)} %bitcast.76, s32[16]{0:T(128)S(1)} %multiply_add_fusion), kind=kOutput, calls=%fused_computation.2 | convolution fusion | flops 60555776 | bytes 5505088 | tf_op jit(solution)/shard_map/qs,qrf->srf/dot_general | solution.py:82
  192.5 8.1 %reshape.250 = bf16[16,2,16,3584]{3,1,0,2:T(2,128)(2,1)} reshape(bf16[32,16,3584]{2,0,1:T(8,128)(2,1)} %convolution_convert_fusion.1) | data formatting | bytes 7340032 | tf_op jit(solution)/shard_map/reshape | solution.py:94
  200.6 7.3 %copy.78 = bf16[16,2,16,3584]{3,1,2,0:T(2,128)(2,1)} copy(bf16[16,2,16,3584]{3,1,0,2:T(2,128)(2,1)} %reshape.250) | data formatting | bytes 7340032 | tf_op jit(solution)/shard_map/reshape | solution.py:94
  207.8 7.4 %all-to-all-start.2 = ((bf16[16,2,16,3584]{3,1,2,0:T(2,128)(2,1)}), bf16[16,2,16,3584]{3,1,2,0:T(2,128)(2,1)}, u32[]{:S(2)}, u32[]{:S(2)}) async-start(bf16[16,2,16,3584]{3,1,2,0:T(2,128)(2,1)} %copy.78), calls=%async_computation.2 | async-start | bytes 7340032 | tf_op jit(solution)/shard_map/all_to_all | solution.py:97
  215.2 0.1 multiply_reduce_fusion
  215.3 0.1 reduce_sum.37
  215.4 0.7 reduce_sum.38
  216.1 4.3 %fusion.11 = f32[2,256,3584]{2,1,0:T(8,128)} fusion(bf16[2,128,3584]{2,1,0:T(8,128)(2,1)S(1)} %bitcast.72, f32[2,256,128]{1,2,0:T(8,128)S(1)} %copy-done.3, f32[2,128]{1,0:T(2,128)S(1)} %mul.31), kind=kOutput, calls=%fused_computation.29 | convolution fusion | flops 469893120 | bytes 9438208 | tf_op jit(solution)/shard_map/blj,bjf->blf/dot_general | solution.py:73
  220.3 0.7 bitcast_convert_fusion.1
  221.1 1.5 copy.86
  222.6 49.1 %all-to-all-done.2 = bf16[16,2,16,3584]{3,1,2,0:T(2,128)(2,1)} async-done(((bf16[16,2,16,3584]{3,1,2,0:T(2,128)(2,1)}), bf16[16,2,16,3584]{3,1,2,0:T(2,128)(2,1)}, u32[]{:S(2)}, u32[]{:S(2)}) %all-to-all-start.2) | async-done | bytes 3670048 | tf_op jit(solution)/shard_map/all_to_all | solution.py:97
  271.7 4.4 %bitcast_convert_fusion = bf16[32,16,3584]{2,0,1:T(8,128)(2,1)S(1)} fusion(bf16[16,2,16,3584]{3,1,2,0:T(2,128)(2,1)} %all-to-all-done.2, pred[16,2,32]{2,1,0:T(4,128)(4,1)S(1)} %and_reduce_fusion), kind=kOutput, calls=%fused_computation | convolution fusion | flops 119275520 | bytes 7341056 | tf_op jit(solution)/shard_map/jce,jcrf->erf/dot_general | solution.py:100
  276.1 3.8 %copy.85 = bf16[32,16,3584]{2,1,0:T(8,128)(2,1)} copy(bf16[32,16,3584]{2,0,1:T(8,128)(2,1)S(1)} %bitcast_convert_fusion) | data formatting | bytes 7340032
  (21 shorter events, 0.1 us)
Async XLA Ops:
  7.2 54.0 %copy-start = (bf16[512,1024]{1,0:T(8,128)(2,1)S(1)}, bf16[512,1024]{1,0:T(8,128)(2,1)}, u32[]{:S(2)}) copy-start(bf16[512,1024]{1,0:T(8,128)(2,1)} %param.7) | copy-start | bytes 3145732
  34.1 17.7 %all-to-all-start = ((bf16[16,2,16,1024]{3,2,1,0:T(8,128)(2,1)}), bf16[16,2,16,1024]{3,2,1,0:T(8,128)(2,1)S(1)}, u32[]{:S(2)}, u32[]{:S(2)}) async-start(bf16[16,2,16,1024]{3,2,1,0:T(8,128)(2,1)} %copy.68), calls=%async_computation | async-start | bytes 2097152 | tf_op jit(solution)/shard_map/all_to_all | solution.py:52
  51.7 7.6 %copy-start.5 = (s32[2,8]{1,0:T(2,128)S(1)}, s32[2,8]{1,0:T(2,128)}, u32[]{:S(2)}) copy-start(s32[2,8]{1,0:T(2,128)} %param.10) | copy-start | bytes 196
  51.7 49.8 %all-to-all-start.1 = ((bf16[16,2,16,3584]{3,2,1,0:T(8,128)(2,1)}), bf16[16,2,16,3584]{3,2,1,0:T(8,128)(2,1)}, u32[]{:S(2)}, u32[]{:S(2)}) async-start(bf16[16,2,16,3584]{3,2,1,0:T(8,128)(2,1)} %copy.73), calls=%async_computation.1 | async-start | bytes 7340032 | tf_op jit(solution)/shard_map/all_to_all | solution.py:51
  59.1 113.0 %all-reduce.3.cloned.1.call-start = ((), (), s32[]{:S(2)}) async-start(), calls=%async_computation.4 | async-start | bytes 1048576 | tf_op jit(solution)/shard_map/psum | solution.py:66
  101.6 7.2 %copy-start.2 = (bf16[512,3584]{1,0:T(8,128)(2,1)S(1)}, bf16[512,3584]{1,0:T(8,128)(2,1)}, u32[]{:S(2)}) copy-start(bf16[512,3584]{1,0:T(8,128)(2,1)} %param.6) | copy-start | bytes 11010052
  108.8 2.1 copy-start.6
  173.4 12.1 %copy-start.3 = (f32[2,256,128]{1,2,0:T(8,128)S(1)}, f32[2,256,128]{1,2,0:T(8,128)}, u32[]{:S(2)}) copy-start(f32[2,256,128]{1,2,0:T(8,128)} %get-tuple-element.20) | copy-start | bytes 786436
  178.4 29.4 %all-to-all-start.3 = ((bf16[16,2,16,1024]{3,1,2,0:T(2,128)(2,1)}), bf16[16,2,16,1024]{3,1,2,0:T(2,128)(2,1)S(1)}, u32[]{:S(2)}, u32[]{:S(2)}) async-start(bf16[16,2,16,1024]{3,1,2,0:T(2,128)(2,1)} %copy.82), calls=%async_computation.3 | async-start | bytes 2097152 | tf_op jit(solution)/shard_map/all_to_all | solution.py:98
  207.8 7.4 %copy-start.4 = (f32[2,256,128]{1,2,0:T(8,128)S(1)}, f32[2,256,128]{1,2,0:T(8,128)}, u32[]{:S(2)}) copy-start(f32[2,256,128]{1,2,0:T(8,128)} %get-tuple-element.21) | copy-start | bytes 786436
  207.8 63.9 %all-to-all-start.2 = ((bf16[16,2,16,3584]{3,1,2,0:T(2,128)(2,1)}), bf16[16,2,16,3584]{3,1,2,0:T(2,128)(2,1)}, u32[]{:S(2)}, u32[]{:S(2)}) async-start(bf16[16,2,16,3584]{3,1,2,0:T(2,128)(2,1)} %copy.78), calls=%async_computation.2 | async-start | bytes 7340032 | tf_op jit(solution)/shard_map/all_to_all | solution.py:97
  271.7 8.3 %copy-start.1 = (bf16[512,1024]{1,0:T(8,128)(2,1)S(1)}, bf16[512,1024]{1,0:T(8,128)(2,1)}, u32[]{:S(2)}) copy-start(bf16[512,1024]{1,0:T(8,128)(2,1)} %param.7) | copy-start | bytes 3145732
Sparse Core Ops, SparseCore 0:
  111.0 61.1 all-reduce.2
where the time goes:
time: 288 us; the launch traced here: 287 us
  waiting for transfers between devices  149 us (52%)
  matrix products  38.3 us (13%)
  local copies, waits for them, and re-layouts  32.5 us (11%)
  starting transfers between devices  29 us (10%)
  blocking collectives  21.6 us (8%)
  between operations  14.2 us (5%)
    psum x1, waiting for transfers between devices, body(): projected, pulled = lax.psum((part_proj, part_pull), 'dp')  61.1 us
    all_to_all x1, waiting for transfers between devices, body(): lax.all_to_all(back_in, 'adapter', split_axis=0, concat_axis=0, tiled=True)  49.1 us
    all_to_all x1, waiting for transfers between devices, body(): lax.all_to_all(send_in, 'adapter', split_axis=0, concat_axis=0, tiled=True)  39.2 us
    all_gather x1, blocking collectives, body(): lax.all_gather(adapter_ids, 'adapter', axis=0, tiled=True)  21.6 us
    reshape x2, local copies, waits for them, and re-layouts, body(): back_in = back_in.reshape(owner_count, CAP, rank_width, -1)  15.4 us
    all_to_all x1, starting transfers between devices, body(): lax.all_to_all(send_in, 'adapter', split_axis=0, concat_axis=0, tiled=True)  7.36 us
    all_to_all x1, starting transfers between devices, body(): lax.all_to_all(back_in, 'adapter', split_axis=0, concat_axis=0, tiled=True)  7.36 us
    all_to_all x1, starting transfers between devices, body(): lax.all_to_all(back_out, 'adapter', split_axis=0, concat_axis=0, tiled=True)  7.14 us
  transfers between devices with their start and end apart: 5, of which 3 were waited for; matrix products, arithmetic and copies ran while one was open for 15% of the time, Pallas kernels for 0%

commit v1 on v0

--- a/solution.py
+++ b/solution.py
@@ -4,6 +4,27 @@
 from jax.sharding import PartitionSpec as P
 
 CAP = 2
+
+
+def laid_out(blocks, dim):
+    blocks = jnp.moveaxis(blocks, 0, dim)
+    shape = blocks.shape
+    return blocks.reshape(*shape[:dim], shape[dim] * shape[dim + 1], *shape[dim + 2 :])
+
+
+def doubled(x, axis):
+    size, index = (lax.axis_size(axis), lax.axis_index(axis))
+    blocks, bit = (x[None], 1)
+    while bit < size:
+        theirs = lax.ppermute(blocks, axis, [(i, i ^ bit) for i in range(size)])
+        low = index & bit == 0
+        blocks = jnp.concatenate([jnp.where(low, blocks, theirs), jnp.where(low, theirs, blocks)])
+        bit *= 2
+    return blocks
+
+
+def doubled_up(array, axis, dim):
+    return laid_out(doubled(array, axis), dim)
 
 
 def body(activations, cotangent, factor_in, factor_out, adapter_ids, router_weights):
@@ -22,9 +43,7 @@
     my_slot = jnp.sum((my_owner[:, None] == my_owner[None, :]) & before, axis=1)
     target = my_owner * CAP + my_slot
     picker = target[:, None] == jnp.arange(slot_count)[None, :]
-    all_ids = lax.all_gather(adapter_ids, "adapter", axis=0, tiled=True).reshape(
-        owner_count, pair_count
-    )
+    all_ids = doubled_up(adapter_ids, "adapter", 0).reshape(owner_count, pair_count)
     all_owner = all_ids // exp_count
     all_slot = jnp.sum(
         (all_owner[:, :, None] == all_owner[:, None, :]) & before[None, :, :], axis=2

time: 288 us -> 287 us (level)
  blocking collectives: 21.6 us -> 0 us
  waiting for transfers between devices: 149 us -> 166 us
  starting transfers between devices: 29 us -> 31.9 us
    all_gather x1 -> x0, blocking collectives: 21.6 us -> none  [body(): lax.all_gather(adapter_ids, 'adapter', axis=0, tiled=True)]
    ppermute x0 -> x4, waiting for transfers between devices: none -> 15 us  [doubled(): theirs = lax.ppermute(blocks, axis, [(i, i ^ bit) for i in range(size)])]
    ppermute x0 -> x4, starting transfers between devices: none -> 2.9 us  [doubled(): theirs = lax.ppermute(blocks, axis, [(i, i ^ bit) for i in range(size)])]
  transfers between devices with their start and end apart: 5 -> 9, of which waited for: 3 -> 7; matrix products, arithmetic and copies ran while one was open for 15% -> 15% of each run, Pallas kernels for 0% -> 0%
where the time goes in v1:
time: 287 us; the launch traced here: 286 us
  waiting for transfers between devices  166 us (58%)
  matrix products  38.3 us (13%)
  local copies, waits for them, and re-layouts  32.5 us (11%)
  starting transfers between devices  31.9 us (11%)
  between operations  14.2 us (5%)
    psum x1, waiting for transfers between devices, body(): projected, pulled = lax.psum((part_proj, part_pull), 'dp')  63.8 us
    all_to_all x1, waiting for transfers between devices, body(): lax.all_to_all(back_in, 'adapter', split_axis=0, concat_axis=0, tiled=True)  49 us
    all_to_all x1, waiting for transfers between devices, body(): lax.all_to_all(send_in, 'adapter', split_axis=0, concat_axis=0, tiled=True)  38.5 us
    reshape x2, local copies, waits for them, and re-layouts, body(): back_in = back_in.reshape(owner_count, CAP, rank_width, -1)  15.4 us
    ppermute x4, waiting for transfers between devices, doubled(): theirs = lax.ppermute(blocks, axis, [(i, i ^ bit) for i in range(size)])  15 us
    all_to_all x1, starting transfers between devices, body(): lax.all_to_all(send_in, 'adapter', split_axis=0, concat_axis=0, tiled=True)  7.36 us
    all_to_all x1, starting transfers between devices, body(): lax.all_to_all(back_in, 'adapter', split_axis=0, concat_axis=0, tiled=True)  7.35 us
    all_to_all x1, starting transfers between devices, body(): lax.all_to_all(back_out, 'adapter', split_axis=0, concat_axis=0, tiled=True)  7.14 us
  transfers between devices with their start and end apart: 9, of which 7 were waited for; matrix products, arithmetic and copies ran while one was open for 15% of the time, Pallas kernels for 0%

profile of v1, /device:TPU:124, one launch (start us, length us, event | category | flops | bytes accessed | tf_op | source)
XLA Modules:
  0.0 285.7 jit_solution(4113061007941485560)
XLA Ops:
  7.2 0.5 collective-permute-start
  7.7 3.4 %collective-permute-done = s32[1,2,8]{2,1,0:T(2,128)S(1)} collective-permute-done((s32[1,2,8]{2,1,0:T(2,128)}, s32[1,2,8]{2,1,0:T(2,128)S(1)}, u32[]{:S(2)}, u32[]{:S(2)}) %collective-permute-start) | collective-permute-done | bytes 96 | tf_op jit(solution)/shard_map/ppermute | solution.py:19
  11.0 0.7 broadcast_select_fusion.7
  11.7 0.6 collective-permute-start.1
  12.3 4.5 %collective-permute-done.1 = s32[2,2,8]{2,1,0:T(2,128)S(1)} collective-permute-done((s32[2,2,8]{2,1,0:T(2,128)S(1)}, s32[2,2,8]{2,1,0:T(2,128)S(1)}, u32[]{:S(2)}, u32[]{:S(2)}) %collective-permute-start.1) | collective-permute-done | bytes 160 | tf_op jit(solution)/shard_map/ppermute | solution.py:19
  16.8 1.3 collective-permute-start.2
  18.1 2.4 collective-permute-done.2
  20.5 0.6 collective-permute-start.3
  21.1 4.6 %collective-permute-done.3 = s32[8,2,8]{2,1,0:T(2,128)S(1)} collective-permute-done((s32[8,2,8]{2,1,0:T(2,128)S(1)}, s32[8,2,8]{2,1,0:T(2,128)S(1)}, u32[]{:S(2)}, u32[]{:S(2)}) %collective-permute-start.3) | collective-permute-done | bytes 544 | tf_op jit(solution)/shard_map/ppermute | solution.py:19
  26.0 0.1 copy.62
  26.1 0.1 iota_compare_fusion
  26.2 0.4 convert_reduce_fusion
  26.7 0.2 and_reduce_fusion
  26.9 2.7 convolution_convert_fusion.4
  29.5 1.5 copy.68
  31.1 6.9 %all-to-all-start = ((bf16[16,2,16,1024]{3,2,1,0:T(8,128)(2,1)}), bf16[16,2,16,1024]{3,2,1,0:T(8,128)(2,1)S(1)}, u32[]{:S(2)}, u32[]{:S(2)}) async-start(bf16[16,2,16,1024]{3,2,1,0:T(8,128)(2,1)} %copy.68), calls=%async_computation | async-start | bytes 2097152 | tf_op jit(solution)/shard_map/all_to_all | solution.py:71
  38.0 6.9 %convolution_convert_fusion = bf16[16,2,16,3584]{3,0,2,1:T(8,128)(2,1)S(1)} fusion(bf16[32,16,3584]{2,1,0:T(8,128)(2,1)} %param.8, pred[16,2,32,1]{2,1,0,3:T(4,128)(4,1)S(1)} %bitcast.83), kind=kOutput, calls=%fused_computation.1 | convolution fusion | flops 119275520 | bytes 7341056 | tf_op jit(solution)/shard_map/jce,erf->jcrf/dot_general | solution.py:60
  44.9 3.8 %copy.73 = bf16[16,2,16,3584]{3,2,1,0:T(8,128)(2,1)} copy(bf16[16,2,16,3584]{3,0,2,1:T(8,128)(2,1)S(1)} %convolution_convert_fusion) | data formatting | bytes 7340032 | tf_op jit(solution)/shard_map/convert_element_type | solution.py:62
  48.8 7.4 %all-to-all-start.1 = ((bf16[16,2,16,3584]{3,2,1,0:T(8,128)(2,1)}), bf16[16,2,16,3584]{3,2,1,0:T(8,128)(2,1)}, u32[]{:S(2)}, u32[]{:S(2)}) async-start(bf16[16,2,16,3584]{3,2,1,0:T(8,128)(2,1)} %copy.73), calls=%async_computation.1 | async-start | bytes 7340032 | tf_op jit(solution)/shard_map/all_to_all | solution.py:70
  56.1 0.2 all-reduce.3.cloned.1.call-start
  56.5 0.2 convert_reduce_fusion.1
  56.7 1.2 convolution_convert_fusion.7
  57.9 0.3 copy.70
  58.2 1.2 convolution_bitcast_fusion.1
  59.4 38.5 %all-to-all-done.1 = bf16[16,2,16,3584]{3,2,1,0:T(8,128)(2,1)} async-done(((bf16[16,2,16,3584]{3,2,1,0:T(8,128)(2,1)}), bf16[16,2,16,3584]{3,2,1,0:T(8,128)(2,1)}, u32[]{:S(2)}, u32[]{:S(2)}) %all-to-all-start.1) | async-done | bytes 3670048 | tf_op jit(solution)/shard_map/all_to_all | solution.py:70
  97.9 6.2 %convolution_convert_fusion.3 = bf16[16,16,3584]{2,0,1:T(8,128)(2,1)S(1)} fusion(bf16[32,16,3584]{2,1,0:T(8,128)(2,1)} %bitcast.11, s32[16]{0:T(128)S(1)} %multiply_add_fusion), kind=kOutput, calls=%fused_computation.4 | convolution fusion | flops 59638272 | bytes 5505088 | tf_op jit(solution)/shard_map/qs,srf->qrf/dot_general | solution.py:75
  104.1 1.0 copy.75
  105.1 2.0 convolution_bitcast_fusion
  107.3 0.1 mul.31
  107.3 63.8 %all-reduce.3.cloned.1.call-done = (f32[2,256,128]{1,2,0:T(8,128)}, f32[2,256,128]{1,2,0:T(8,128)}) async-done(((f32[2,256,128]{1,2,0:T(8,128)}, f32[2,256,128]{1,2,0:T(8,128)}), (f32[2,256,128]{1,2,0:T(8,128)}, f32[2,256,128]{1,2,0:T(8,128)})) %all-reduce.3.cloned.1.call-update) | async-done | bytes 524304 | tf_op jit(solution)/shard_map/psum | solution.py:85
  171.1 1.3 convolution_convert_fusion.6
  172.4 0.6 convolution_convert_fusion.5
  173.0 1.2 reshape.248
  174.2 3.2 %copy.82 = bf16[16,2,16,1024]{3,1,2,0:T(2,128)(2,1)} copy(bf16[16,2,16,1024]{3,1,0,2:T(2,128)(2,1)} %reshape.248) | data formatting | bytes 2097152 | tf_op jit(solution)/shard_map/reshape | solution.py:114
  177.4 7.1 %all-to-all-start.3 = ((bf16[16,2,16,1024]{3,1,2,0:T(2,128)(2,1)}), bf16[16,2,16,1024]{3,1,2,0:T(2,128)(2,1)S(1)}, u32[]{:S(2)}, u32[]{:S(2)}) async-start(bf16[16,2,16,1024]{3,1,2,0:T(2,128)(2,1)} %copy.82), calls=%async_computation.3 | async-start | bytes 2097152 | tf_op jit(solution)/shard_map/all_to_all | solution.py:117
  184.5 2.7 convolution_convert_fusion.2
  187.3 4.2 %convolution_convert_fusion.1 = bf16[32,16,3584]{2,0,1:T(8,128)(2,1)} fusion(bf16[16,16,3584]{2,1,0:T(8,128)(2,1)S(1)} %bitcast.78, s32[16]{0:T(128)S(1)} %multiply_add_fusion), kind=kOutput, calls=%fused_computation.2 | convolution fusion | flops 60555776 | bytes 5505088 | tf_op jit(solution)/shard_map/qs,qrf->srf/dot_general | solution.py:101
  191.4 8.1 %reshape.246 = bf16[16,2,16,3584]{3,1,0,2:T(2,128)(2,1)} reshape(bf16[32,16,3584]{2,0,1:T(8,128)(2,1)} %convolution_convert_fusion.1) | data formatting | bytes 7340032 | tf_op jit(solution)/shard_map/reshape | solution.py:113
  199.5 7.3 %copy.78 = bf16[16,2,16,3584]{3,1,2,0:T(2,128)(2,1)} copy(bf16[16,2,16,3584]{3,1,0,2:T(2,128)(2,1)} %reshape.246) | data formatting | bytes 7340032 | tf_op jit(solution)/shard_map/reshape | solution.py:113
  206.8 7.4 %all-to-all-start.2 = ((bf16[16,2,16,3584]{3,1,2,0:T(2,128)(2,1)}), bf16[16,2,16,3584]{3,1,2,0:T(2,128)(2,1)}, u32[]{:S(2)}, u32[]{:S(2)}) async-start(bf16[16,2,16,3584]{3,1,2,0:T(2,128)(2,1)} %copy.78), calls=%async_computation.2 | async-start | bytes 7340032 | tf_op jit(solution)/shard_map/all_to_all | solution.py:116
  214.2 0.1 multiply_reduce_fusion
  214.4 0.7 reduce_sum.38
  215.0 4.3 %fusion.11 = f32[2,256,3584]{2,1,0:T(8,128)} fusion(bf16[2,128,3584]{2,1,0:T(8,128)(2,1)S(1)} %bitcast.74, f32[2,256,128]{1,2,0:T(8,128)S(1)} %copy-done.3, f32[2,128]{1,0:T(2,128)S(1)} %mul.31), kind=kOutput, calls=%fused_computation.29 | convolution fusion | flops 469893120 | bytes 9438208 | tf_op jit(solution)/shard_map/blj,bjf->blf/dot_general | solution.py:92
  219.3 0.7 bitcast_convert_fusion.1
  220.0 1.5 copy.86
  221.6 49.0 %all-to-all-done.2 = bf16[16,2,16,3584]{3,1,2,0:T(2,128)(2,1)} async-done(((bf16[16,2,16,3584]{3,1,2,0:T(2,128)(2,1)}), bf16[16,2,16,3584]{3,1,2,0:T(2,128)(2,1)}, u32[]{:S(2)}, u32[]{:S(2)}) %all-to-all-start.2) | async-done | bytes 3670048 | tf_op jit(solution)/shard_map/all_to_all | solution.py:116
  270.6 4.4 %bitcast_convert_fusion = bf16[32,16,3584]{2,0,1:T(8,128)(2,1)S(1)} fusion(bf16[16,2,16,3584]{3,1,2,0:T(2,128)(2,1)} %all-to-all-done.2, pred[16,2,32]{2,1,0:T(4,128)(4,1)S(1)} %and_reduce_fusion), kind=kOutput, calls=%fused_computation | convolution fusion | flops 119275520 | bytes 7341056 | tf_op jit(solution)/shard_map/jce,jcrf->erf/dot_general | solution.py:119
  275.0 3.8 %copy.85 = bf16[32,16,3584]{2,1,0:T(8,128)(2,1)} copy(bf16[32,16,3584]{2,0,1:T(8,128)(2,1)S(1)} %bitcast_convert_fusion) | data formatting | bytes 7340032
  (36 shorter events, 0.6 us)
Async XLA Ops:
  7.2 51.0 %copy-start = (bf16[512,1024]{1,0:T(8,128)(2,1)S(1)}, bf16[512,1024]{1,0:T(8,128)(2,1)}, u32[]{:S(2)}) copy-start(bf16[512,1024]{1,0:T(8,128)(2,1)} %param.7) | copy-start | bytes 3145732
  7.2 3.9 %collective-permute-start = (s32[1,2,8]{2,1,0:T(2,128)}, s32[1,2,8]{2,1,0:T(2,128)S(1)}, u32[]{:S(2)}, u32[]{:S(2)}) collective-permute-start(s32[1,2,8]{2,1,0:T(2,128)} %bitcast.84), channel_id=1, source_target_pairs={{0,1},{1,0},{2,3},{3,2},{4,5},{5,4},{6,7},{7,6},{8,9},{9,8},{10,11... | collective-permute-start | bytes 200 | tf_op jit(solution)/shard_map/ppermute | solution.py:19
  11.7 5.1 %collective-permute-start.1 = (s32[2,2,8]{2,1,0:T(2,128)S(1)}, s32[2,2,8]{2,1,0:T(2,128)S(1)}, u32[]{:S(2)}, u32[]{:S(2)}) collective-permute-start(s32[2,2,8]{2,1,0:T(2,128)S(1)} %pad_add_fusion.3), channel_id=1, source_target_pairs={{0,2},{1,3},{2,0},{3,1},{4,6},{5,7},{6,4},{7,5},{8,10},{9,11},{10,... | collective-permute-start | bytes 392 | tf_op jit(solution)/shard_map/ppermute | solution.py:19
  16.8 3.7 %collective-permute-start.2 = (s32[4,2,8]{2,1,0:T(2,128)S(1)}, s32[4,2,8]{2,1,0:T(2,128)S(1)}, u32[]{:S(2)}, u32[]{:S(2)}) collective-permute-start(s32[4,2,8]{2,1,0:T(2,128)S(1)} %pad_add_fusion.2), channel_id=1, source_target_pairs={{0,4},{1,5},{2,6},{3,7},{4,0},{5,1},{6,2},{7,3},{8,12},{9,13},{10,... | collective-permute-start | bytes 776 | tf_op jit(solution)/shard_map/ppermute | solution.py:19
  20.5 5.2 %collective-permute-start.3 = (s32[8,2,8]{2,1,0:T(2,128)S(1)}, s32[8,2,8]{2,1,0:T(2,128)S(1)}, u32[]{:S(2)}, u32[]{:S(2)}) collective-permute-start(s32[8,2,8]{2,1,0:T(2,128)S(1)} %pad_add_fusion.1), channel_id=1, source_target_pairs={{0,8},{1,9},{2,10},{3,11},{4,12},{5,13},{6,14},{7,15},{8,0},{9,1},... | collective-permute-start | bytes 1544 | tf_op jit(solution)/shard_map/ppermute | solution.py:19
  31.1 17.7 %all-to-all-start = ((bf16[16,2,16,1024]{3,2,1,0:T(8,128)(2,1)}), bf16[16,2,16,1024]{3,2,1,0:T(8,128)(2,1)S(1)}, u32[]{:S(2)}, u32[]{:S(2)}) async-start(bf16[16,2,16,1024]{3,2,1,0:T(8,128)(2,1)} %copy.68), calls=%async_computation | async-start | bytes 2097152 | tf_op jit(solution)/shard_map/all_to_all | solution.py:71
  48.8 7.6 %copy-start.6 = (s32[2,8]{1,0:T(2,128)S(1)}, s32[2,8]{1,0:T(2,128)}, u32[]{:S(2)}) copy-start(s32[2,8]{1,0:T(2,128)} %param.10) | copy-start | bytes 196
  48.8 49.1 %all-to-all-start.1 = ((bf16[16,2,16,3584]{3,2,1,0:T(8,128)(2,1)}), bf16[16,2,16,3584]{3,2,1,0:T(8,128)(2,1)}, u32[]{:S(2)}, u32[]{:S(2)}) async-start(bf16[16,2,16,3584]{3,2,1,0:T(8,128)(2,1)} %copy.73), calls=%async_computation.1 | async-start | bytes 7340032 | tf_op jit(solution)/shard_map/all_to_all | solution.py:70
  56.1 115.0 %all-reduce.3.cloned.1.call-start = ((), (), s32[]{:S(2)}) async-start(), calls=%async_computation.4 | async-start | bytes 1048576 | tf_op jit(solution)/shard_map/psum | solution.py:85
  97.9 7.2 %copy-start.2 = (bf16[512,3584]{1,0:T(8,128)(2,1)S(1)}, bf16[512,3584]{1,0:T(8,128)(2,1)}, u32[]{:S(2)}) copy-start(bf16[512,3584]{1,0:T(8,128)(2,1)} %param.6) | copy-start | bytes 11010052
  105.1 2.1 copy-start.5
  172.4 12.1 %copy-start.3 = (f32[2,256,128]{1,2,0:T(8,128)S(1)}, f32[2,256,128]{1,2,0:T(8,128)}, u32[]{:S(2)}) copy-start(f32[2,256,128]{1,2,0:T(8,128)} %get-tuple-element.20) | copy-start | bytes 786436
  177.4 29.4 %all-to-all-start.3 = ((bf16[16,2,16,1024]{3,1,2,0:T(2,128)(2,1)}), bf16[16,2,16,1024]{3,1,2,0:T(2,128)(2,1)S(1)}, u32[]{:S(2)}, u32[]{:S(2)}) async-start(bf16[16,2,16,1024]{3,1,2,0:T(2,128)(2,1)} %copy.82), calls=%async_computation.3 | async-start | bytes 2097152 | tf_op jit(solution)/shard_map/all_to_all | solution.py:117
  206.8 7.4 %copy-start.4 = (f32[2,256,128]{1,2,0:T(8,128)S(1)}, f32[2,256,128]{1,2,0:T(8,128)}, u32[]{:S(2)}) copy-start(f32[2,256,128]{1,2,0:T(8,128)} %get-tuple-element.21) | copy-start | bytes 786436
  206.8 63.8 %all-to-all-start.2 = ((bf16[16,2,16,3584]{3,1,2,0:T(2,128)(2,1)}), bf16[16,2,16,3584]{3,1,2,0:T(2,128)(2,1)}, u32[]{:S(2)}, u32[]{:S(2)}) async-start(bf16[16,2,16,3584]{3,1,2,0:T(2,128)(2,1)} %copy.78), calls=%async_computation.2 | async-start | bytes 7340032 | tf_op jit(solution)/shard_map/all_to_all | solution.py:116
  270.6 8.3 %copy-start.1 = (bf16[512,1024]{1,0:T(8,128)(2,1)S(1)}, bf16[512,1024]{1,0:T(8,128)(2,1)}, u32[]{:S(2)}) copy-start(bf16[512,1024]{1,0:T(8,128)(2,1)} %param.7) | copy-start | bytes 3145732
Sparse Core Ops, SparseCore 0:
  107.3 63.7 all-reduce.2
